TPU v7x, 32 devices: a whole 2x2x4 slice. The times are simulated.
32 devices in a mesh: chan: 16 (over z, y, core), slot: 2 (over x).
Axes of the slice: x: 2, y: 2, z: 4, core: 2. Of those that a mesh axis runs over, the one named last changes fastest.
Arguments:
- measured_real: float32 [2, 16, 1770], P('slot', 'chan'), may hold values from -60 to 60
- measured_imaginary: float32 [2, 16, 1770], P('slot', 'chan'), may hold values from -60 to 60
- measured_weight: float32 [2, 16, 1770], P('slot', 'chan'), may hold values from 0.3 to 3
- baseline_vectors: float32 [2, 3, 1770], P('slot'), may hold values from -120 to 120
- antenna_pairs: int32 [2, 1770], replicated, may hold values from 0 to 59, as said below
- directions: float32 [3, 200], replicated, may hold values from -0.12 to 0.12
- direction_flux: float32 [16, 200], P('chan'), may hold values from 0.2 to 2
- channel_frequency: float32 [16], P('chan'), may hold values from 1.1 to 1.9
- electron_content_start: float32 [2, 60, 200], P('slot'), may hold values from -6 to 6
- pierce_station_direction: int32 [2, 12000], P('slot'), may hold values from 0 to 11999, each once within a row
- eigen_basis: float32 [12000, 2048], P('chan'), may hold values from -0.0546875 to 0.0546875
- eigen_weight: float32 [2048], replicated, may hold values from 0.1 to 1
Outputs:
- tec_final: float32 [2, 60, 200], P('slot')
- coefficients: float32 [2, 2048], P('slot')
- final_residual_real: float32 [2, 16, 1770], P('slot', 'chan')
- final_residual_imaginary: float32 [2, 16, 1770], P('slot', 'chan')
Inputs may be any that keep to these rules, and one draw needn't show every extreme that they name: `antenna_pairs`: each column is a pair of two different stations, and the 1770 columns hold every unordered pair of stations exactly once. `pierce_station_direction`: each row names every station-direction pair exactly once.
All inputs are finite; a program needn't handle non-finite values.
Results may differ from a plain program's by a relative error of at most 0.00018.
Values sent between devices are 32-bit elements; how exact they have to be, the bound alone decides.
A program may use at most 64 MiB of HBM per device.

v0:
```python
import jax
import jax.numpy as jnp
from jax import lax
from jax.sharding import PartitionSpec as P

ITERS = 4


HIGHEST = lax.Precision.HIGHEST
TEC_PHASE = -0.8448
SMOOTHING = 0.5
TWO_PI = 6.283185307179586


def padded_2(cells, sides, width):
    for axis, dim in sides:
        count = lax.axis_size(axis)
        ends = count - 1
        head = lax.slice_in_dim(cells, 0, width, axis=dim)
        tail = lax.slice_in_dim(cells, cells.shape[dim] - width, cells.shape[dim], axis=dim)
        cells = jnp.concatenate(
            [
                lax.ppermute(tail, axis, [(i, (i + 1) % count) for i in range(ends)]),
                cells,
                lax.ppermute(head, axis, [((i + 1) % count, i) for i in range(ends)]),
            ],
            axis=dim,
        )
    return cells


def station_polarity(antenna_pairs, station_list):
    station_numbers = jnp.arange(station_list, dtype=jnp.int32)[:, None]
    first_match = (antenna_pairs[0][None, :] == station_numbers).astype(jnp.float32)
    second_match = (antenna_pairs[1][None, :] == station_numbers).astype(jnp.float32)
    return (first_match - second_match, first_match + second_match)


def pair_terms(
    vis_real, vis_imag, weights, coords, frequency, fluxes, tec_slot, signed_terms, directions
):
    geometry = TWO_PI * frequency * jnp.dot(coords.T, directions, precision=HIGHEST)
    station_phase = TEC_PHASE / frequency * tec_slot
    phases = geometry + jnp.dot(signed_terms.T, station_phase, precision=HIGHEST)
    model_real = fluxes[None, :] * jnp.cos(phases)
    model_imag = fluxes[None, :] * jnp.sin(phases)
    leftover_real = vis_real - jnp.sum(model_real, axis=1)
    leftover_imaginary = vis_imag - jnp.sum(model_imag, axis=1)
    projected = weights[:, None] * (
        model_real * leftover_imaginary[:, None] - model_imag * leftover_real[:, None]
    )
    numerator = TEC_PHASE / frequency * jnp.dot(signed_terms, projected, precision=HIGHEST)
    return (numerator, leftover_real, leftover_imaginary)


def slot_smooth(values, padded):
    shard_slots = values.shape[0]
    first_slot = lax.axis_index("slot") * shard_slots
    position = first_slot + jnp.arange(shard_slots, dtype=jnp.int32)
    slot_total = shard_slots * lax.axis_size("slot")
    neighbours = (position > 0).astype(jnp.float32) + (position < slot_total - 1).astype(
        jnp.float32
    )
    return (values + SMOOTHING * (padded[:-2] + padded[2:])) / (1.0 + SMOOTHING * neighbours)[
        :, None
    ]


def smooth_coefficients(values):
    padded = padded_2(values, (("slot", 0),), 1)
    return slot_smooth(values, padded)


def reduce_normals(values):
    return lax.psum(values, "chan")


def updated_field(tec_flat, numer_sum, denom_sum):
    return tec_flat + numer_sum / denom_sum


def select_points(field, one_station, one_direction):
    rows = jnp.einsum("trs,tsd->trd", one_station, field, precision=HIGHEST)
    return jnp.sum(rows * one_direction, axis=2)


def place_points(values, one_station, one_direction):
    return jnp.einsum(
        "trs,trd->tsd", one_station, values[:, :, None] * one_direction, precision=HIGHEST
    )


def per_device(
    measured_real,
    measured_imaginary,
    measured_weight,
    baseline_vectors,
    antenna_pairs,
    directions,
    direction_flux,
    channel_frequency,
    electron_content_start,
    pierce_station_direction,
    eigen_basis,
    eigen_weight,
):
    shard_slots, shard_channels, baseline_list = measured_real.shape
    station_list = electron_content_start.shape[1]
    sources = electron_content_start.shape[2]
    block_rows = eigen_basis.shape[0]
    signed_terms, station_touches = station_polarity(antenna_pairs, station_list)
    tec_scale = TEC_PHASE / channel_frequency
    station_weight = jnp.einsum("sb,tfb->tfs", station_touches, measured_weight, precision=HIGHEST)
    denominator = jnp.einsum(
        "tfs,fd->tsd",
        station_weight * (tec_scale * tec_scale)[None, :, None],
        direction_flux * direction_flux,
        precision=HIGHEST,
    )
    own_map = lax.dynamic_slice_in_dim(
        pierce_station_direction, lax.axis_index("chan") * block_rows, block_rows, 1
    )
    station_of = own_map // sources
    direction_of = own_map % sources
    one_station = (
        station_of[:, :, None] == jnp.arange(station_list, dtype=jnp.int32)[None, None, :]
    ).astype(jnp.float32)
    one_direction = (
        direction_of[:, :, None] == jnp.arange(sources, dtype=jnp.int32)[None, None, :]
    ).astype(jnp.float32)
    denom_sum = reduce_normals(denominator.reshape(shard_slots, -1))
    tec_flat = electron_content_start.reshape(shard_slots, -1)
    pair_total = shard_slots * shard_channels
    smooth = None
    leftover_real = None
    leftover_imaginary = None
    for iteration in range(ITERS):
        current = tec_flat

        def pair_step(flat_index):
            slot_index = flat_index // shard_channels
            channel = flat_index % shard_channels
            tec_slot = current[slot_index].reshape(station_list, sources)
            return pair_terms(
                measured_real[slot_index, channel],
                measured_imaginary[slot_index, channel],
                measured_weight[slot_index, channel],
                baseline_vectors[slot_index],
                channel_frequency[channel],
                direction_flux[channel],
                tec_slot,
                signed_terms,
                directions,
            )

        numerator, leftover_real, leftover_imaginary = lax.map(
            pair_step, jnp.arange(pair_total, dtype=jnp.int32)
        )
        numerator = jnp.sum(numerator.reshape(shard_slots, shard_channels, -1), axis=1)
        numer_sum = reduce_normals(numerator)
        update = updated_field(current, numer_sum, denom_sum)
        target = select_points(
            update.reshape(shard_slots, station_list, sources), one_station, one_direction
        )
        partial_value = eigen_weight[None, :] * jnp.dot(target, eigen_basis, precision=HIGHEST)
        raw = lax.psum(partial_value, "chan")
        smooth = smooth_coefficients(raw)
        screen_own = jnp.dot(smooth, eigen_basis.T, precision=HIGHEST)
        placed = place_points(screen_own, one_station, one_direction).reshape(shard_slots, -1)
        tec_flat = lax.psum(placed, "chan")
    final_residual_real = leftover_real.reshape(shard_slots, shard_channels, baseline_list)
    final_residual_imaginary = leftover_imaginary.reshape(
        shard_slots, shard_channels, baseline_list
    )
    return (
        tec_flat.reshape(shard_slots, station_list, sources),
        smooth,
        final_residual_real,
        final_residual_imaginary,
    )


def solution(mesh):
    in_specs = (
        P("slot", "chan", None),
        P("slot", "chan", None),
        P("slot", "chan", None),
        P("slot", None, None),
        P(),
        P(),
        P("chan", None),
        P("chan"),
        P("slot", None, None),
        P("slot", None),
        P("chan", None),
        P(),
    )
    out_specs = (
        P("slot", None, None),
        P("slot", None),
        P("slot", "chan", None),
        P("slot", "chan", None),
    )
    return jax.shard_map(
        per_device, mesh=mesh, in_specs=in_specs, out_specs=out_specs, check_vma=False
    )
```

profile of v0, /device:TPU:0, one launch (start us, length us, event | category | flops | bytes accessed | tf_op | source)
XLA Modules:
  0.0 784.9 jit_solution(13449369649280400998)
XLA Ops:
  16.9 6.5 fusion.21
  23.4 7.0 fusion.32
  32.2 90.9 %all-reduce.3.cloned.1.call-done = (f32[1,12000]{1,0:T(1,128)}, f32[1,12000]{1,0:T(1,128)}) async-done(((f32[1,12000]{1,0:T(1,128)}, f32[1,12000]{1,0:T(1,128)}), (f32[1,12000]{1,0:T(1,128)}, f32[1,12000]{1,0:T(1,128)})) %all-reduce.3.cloned.1.call-update) | async-done | bytes 96016 | tf_op jit(solution)/shard_map/psum | solution.py:75
  124.8 5.7 fusion.155
  130.5 31.0 %psum.93 = f32[1,2048]{1,0:T(1,128)S(1)} all-reduce(f32[1,2048]{1,0:T(1,128)S(1)} %bitcast.100), channel_id=1, replica_groups=mesh['chan'=16,'slot'=2] {'chan'}, use_global_device_ids=true, to_apply=%region_5.6 | all-reduce | flops 2048 | bytes 16384 | tf_op jit(solution)/shard_map/psum | solution.py:166
  162.8 4.5 collective-permute-start
  168.7 7.1 convolution_reduce_fusion.3
  176.5 57.9 %psum.94 = f32[1,12000]{1,0:T(1,128)S(1)} all-reduce(f32[1,12000]{1,0:T(1,128)S(1)} %reshape.689), channel_id=1, replica_groups=mesh['chan'=16,'slot'=2] {'chan'}, use_global_device_ids=true, to_apply=%region_6.7 | all-reduce | flops 12000 | bytes 96000 | tf_op jit(solution)/shard_map/psum | solution.py:170
  234.7 6.5 fusion.23
  241.2 6.8 fusion.35
  248.1 57.7 %psum.95 = f32[1,12000]{1,0:T(1,128)S(1)} all-reduce(f32[1,12000]{1,0:T(1,128)S(1)} %reduce_sum.150), channel_id=1, replica_groups=mesh['chan'=16,'slot'=2] {'chan'}, use_global_device_ids=true, to_apply=%region_9.10 | all-reduce | flops 12000 | bytes 96000 | tf_op jit(solution)/shard_map/psum | solution.py:75
  306.7 5.7 fusion.156
  312.4 30.0 %psum.96 = f32[1,2048]{1,0:T(1,128)S(1)} all-reduce(f32[1,2048]{1,0:T(1,128)S(1)} %bitcast.101), channel_id=1, replica_groups=mesh['chan'=16,'slot'=2] {'chan'}, use_global_device_ids=true, to_apply=%region_11.12 | all-reduce | flops 2048 | bytes 16384 | tf_op jit(solution)/shard_map/psum | solution.py:166
  343.7 4.5 collective-permute-start.2
  349.6 7.1 convolution_reduce_fusion.2
  357.4 58.1 %psum.97 = f32[1,12000]{1,0:T(1,128)S(1)} all-reduce(f32[1,12000]{1,0:T(1,128)S(1)} %reshape.692), channel_id=1, replica_groups=mesh['chan'=16,'slot'=2] {'chan'}, use_global_device_ids=true, to_apply=%region_12.13 | all-reduce | flops 12000 | bytes 96000 | tf_op jit(solution)/shard_map/psum | solution.py:170
  415.7 6.5 fusion.25
  422.3 6.8 fusion.38
  429.2 57.7 %psum.98 = f32[1,12000]{1,0:T(1,128)S(1)} all-reduce(f32[1,12000]{1,0:T(1,128)S(1)} %reduce_sum.154), channel_id=1, replica_groups=mesh['chan'=16,'slot'=2] {'chan'}, use_global_device_ids=true, to_apply=%region_15.16 | all-reduce | flops 12000 | bytes 96000 | tf_op jit(solution)/shard_map/psum | solution.py:75
  487.7 5.7 fusion.157
  493.5 30.0 %psum.99 = f32[1,2048]{1,0:T(1,128)S(1)} all-reduce(f32[1,2048]{1,0:T(1,128)S(1)} %bitcast.102), channel_id=1, replica_groups=mesh['chan'=16,'slot'=2] {'chan'}, use_global_device_ids=true, to_apply=%region_17.18 | all-reduce | flops 2048 | bytes 16384 | tf_op jit(solution)/shard_map/psum | solution.py:166
  524.7 4.5 collective-permute-start.4
  530.6 7.1 convolution_reduce_fusion.1
  538.4 57.9 %psum.100 = f32[1,12000]{1,0:T(1,128)S(1)} all-reduce(f32[1,12000]{1,0:T(1,128)S(1)} %reshape.695), channel_id=1, replica_groups=mesh['chan'=16,'slot'=2] {'chan'}, use_global_device_ids=true, to_apply=%region_18.19 | all-reduce | flops 12000 | bytes 96000 | tf_op jit(solution)/shard_map/psum | solution.py:170
  596.6 6.5 fusion.27
  603.1 6.8 fusion.41
  610.1 57.7 %psum.101 = f32[1,12000]{1,0:T(1,128)S(1)} all-reduce(f32[1,12000]{1,0:T(1,128)S(1)} %reduce_sum.158), channel_id=1, replica_groups=mesh['chan'=16,'slot'=2] {'chan'}, use_global_device_ids=true, to_apply=%region_21.22 | all-reduce | flops 12000 | bytes 96000 | tf_op jit(solution)/shard_map/psum | solution.py:75
  668.7 5.7 fusion.158
  674.4 30.0 %psum.102 = f32[1,2048]{1,0:T(1,128)S(1)} all-reduce(f32[1,2048]{1,0:T(1,128)S(1)} %bitcast.103), channel_id=1, replica_groups=mesh['chan'=16,'slot'=2] {'chan'}, use_global_device_ids=true, to_apply=%region_23.24 | all-reduce | flops 2048 | bytes 16384 | tf_op jit(solution)/shard_map/psum | solution.py:166
  705.7 4.5 collective-permute-start.6
  711.6 7.1 convolution_reduce_fusion
  719.3 57.7 %psum.103 = f32[1,60,200]{2,1,0:T(8,128)S(1)} all-reduce(f32[1,60,200]{2,1,0:T(8,128)S(1)} %convolution_bitcast_fusion), channel_id=1, replica_groups=mesh['chan'=16,'slot'=2] {'chan'}, use_global_device_ids=true, to_apply=%region_24.25 | all-reduce | flops 12000 | bytes 96000 | tf_op jit(solution)/shard_map/psum | solution.py:170
  (88 shorter events, 29.6 us)
Async XLA Ops:
  7.2 7.6 copy-start
  7.2 9.7 %copy-start.3 = (f32[1,200]{1,0:T(1,128)S(1)}, f32[1,200]{1,0:T(1,128)}, u32[]{:S(2)}) copy-start(f32[1,200]{1,0:T(1,128)} %param.18) | copy-start | bytes 2404
  7.2 115.9 %all-reduce.3.cloned.1.call-start = ((), (), s32[]{:S(2)}) async-start(), calls=%async_computation | async-start | bytes 192512 | tf_op jit(solution)/shard_map/psum | solution.py:75
  124.8 5.8 copy-start.2
  161.5 5.9 collective-permute-start.1
  162.8 5.9 collective-permute-start
  241.2 64.7 %copy-start.1 = (f32[1,12000]{1,0:T(1,128)S(1)}, f32[1,12000]{1,0:T(1,128)}, u32[]{:S(2)}) copy-start(f32[1,12000]{1,0:T(1,128)} %get-tuple-element.141) | copy-start | bytes 144004
  342.4 5.9 collective-permute-start.3
  343.7 5.9 collective-permute-start.2
  523.4 5.9 collective-permute-start.5
  524.7 5.9 collective-permute-start.4
  668.6 41.6 %copy-start.5 = (f32[1,1,1770]{2,1,0:T(1,128)S(1)}, f32[1,1,1770]{2,1,0:T(1,128)}, u32[]{:S(2)}) copy-start(f32[1,1,1770]{2,1,0:T(1,128)} %param.12) | copy-start | bytes 21244
  668.6 41.6 %copy-start.6 = (f32[1,1,1770]{2,1,0:T(1,128)S(1)}, f32[1,1,1770]{2,1,0:T(1,128)}, u32[]{:S(2)}) copy-start(f32[1,1,1770]{2,1,0:T(1,128)} %param.13) | copy-start | bytes 21244
  704.4 6.5 collective-permute-start.7
  705.7 5.9 collective-permute-start.6
  711.6 7.1 copy-start.4
Sparse Core Ops, SparseCore 0:
  31.3 91.7 all-reduce.2
where the time goes:
time: 794 us; the launch traced here: 785 us
  blocking collectives  526 us (66%)
  matrix products  112 us (14%)
  waiting for transfers between devices  95.7 us (12%)
  starting transfers between devices  23.4 us (3%)
  between operations  15.8 us (2%)
    psum x4, blocking collectives, per_device(): tec_flat = lax.psum(placed, 'chan')  232 us
    psum x3, blocking collectives, reduce_normals(): return lax.psum(values, 'chan')  173 us
    psum x4, blocking collectives, per_device(): raw = lax.psum(partial_value, 'chan')  121 us
    psum x1, waiting for transfers between devices, reduce_normals(): return lax.psum(values, 'chan')  90.9 us
    dot_general x4, matrix products, per_device(): screen_own = jnp.dot(smooth, eigen_basis.T, precision=HIGHEST)  28.3 us
    dot_general x4, matrix products, pair_terms(): jnp.dot(signed_terms, projected, precision=HIGHEST)  27.4 us
    dot_general x4, matrix products, pair_terms(): jnp.dot(signed_terms.T, station_phase, precision=HIGHEST)  26 us
    dot_general x4, matrix products, per_device(): jnp.dot(target, eigen_basis, precision=HIGHEST)  23 us
  transfers between devices with their start and end apart: 9, of which 5 were waited for; matrix products, arithmetic and copies ran while one was open for 0% of the time, Pallas kernels for 0%

commit v1 on v0

v1 whole, which is shorter than its diff:
```python
import functools

import jax
import jax.numpy as jnp
from jax import lax
from jax.experimental import pallas as pl
from jax.experimental.pallas import tpu as pltpu
from jax.sharding import PartitionSpec as P

ITERS = 4
TEC_PHASE = -0.8448
SMOOTHING = 0.5
TWO_PI = 6.283185307179586
LANES = 128
TILE = 256

COS_TERMS = ()
SIN_TERMS = ()


def _fit():
    import numpy as np

    nodes = 4000
    theta = np.pi * (np.arange(nodes) + 0.5) / nodes
    u = 0.125 * (1.0 + np.cos(theta))
    r = np.sqrt(u)
    out = []
    for values in (np.cos(2 * np.pi * r), np.sin(2 * np.pi * r) / r):
        cheb = np.polynomial.chebyshev.Chebyshev.fit(u, values, 7, domain=[0.0, 0.25])
        coefs = cheb.convert(kind=np.polynomial.Polynomial).coef
        out.append(tuple(float(np.float32(c)) for c in coefs))
    return out


COS_TERMS, SIN_TERMS = _fit()


def round_up(value, unit):
    return -(-value // unit) * unit


def horner(terms, u):
    acc = jnp.full_like(u, terms[-1])
    for term in terms[-2::-1]:
        acc = acc * u + term
    return acc


def split3(x):
    hi = x.astype(jnp.bfloat16)
    rest = x - hi.astype(jnp.float32)
    mid = rest.astype(jnp.bfloat16)
    low = (rest - mid.astype(jnp.float32)).astype(jnp.bfloat16)
    return hi, mid, low


def dot32(a, b, ca, cb):
    return lax.dot_general(a, b, (((ca,), (cb,)), ((), ())), preferred_element_type=jnp.float32)


def solve_kernel(
    geo,
    vr_ref, vi_ref, w_ref, bv_ref, pairs_ref, cols_ref, flux_ref, freq_ref, tec0_ref,
    smap_ref, dmap_ref, basis_ref, ew_ref,
    tec_out, coef_out, rr_out, ri_out,
    visr, visi, wt, geom, sign3, sgn, fluxb, phase, mre, mim, phi, plo,
    tec, tec3, acc, den, basis, ones3, oned, onedf, target, place,
    stage, abuf, bbuf, craw, cbuf, dbuf, ebuf, fbuf,
    basis_sem, send_sem, recv_sem, csend, crecv,
):
    n, slots, tiles, base_n, srcs, drows, sp, dp, cr, rows, rpad, kk, cw = geo
    me = lax.axis_index("chan")
    slot = lax.axis_index("slot")
    offs = sorted({1 % slots, (slots - 1) % slots} - {0})

    def peer(k):
        return lax.rem(me + k, n)

    whole8 = rows // 8 * 8
    load = pltpu.make_async_copy(basis_ref, basis, basis_sem)
    load.start()

    barrier = pltpu.get_barrier_semaphore()

    def greet(k, c):
        pl.semaphore_signal(
            barrier, inc=1, device_id={"chan": peer(k), "slot": slot},
            device_id_type=pl.DeviceIdType.MESH,
        )
        return c

    lax.fori_loop(1, n, greet, 0)
    for off in offs:

        def greet_far(k, c, off=off):
            pl.semaphore_signal(
                barrier, inc=1,
                device_id={"chan": peer(k), "slot": lax.rem(slot + off, slots)},
                device_id_type=pl.DeviceIdType.MESH,
            )
            return c

        lax.fori_loop(0, n, greet_far, 0)

    freq = freq_ref[...]
    scale = TEC_PHASE / freq
    turn_scale = (TEC_PHASE / TWO_PI) / freq
    fluxb[...] = jnp.broadcast_to(cols_ref[:, 0:1], (drows, TILE))
    station = lax.broadcasted_iota(jnp.int32, (sp, TILE), 0)
    weight_sum = jnp.zeros((sp, 1), jnp.float32)
    for j in range(tiles):
        lo = j * TILE
        width = min(TILE, base_n - lo)
        for dst, src in ((visr, vr_ref[0]), (visi, vi_ref[0]), (wt, w_ref[0])):
            if width < TILE:
                dst[j] = jnp.zeros((1, TILE), jnp.float32)
            dst[j, :, 0:width] = src[:, lo : lo + width]
        pairs = pairs_ref[:, lo : lo + TILE]
        first = (pairs[0:1, :] == station).astype(jnp.float32)
        second = (pairs[1:2, :] == station).astype(jnp.float32)
        polarity = first - second
        weight_sum = weight_sum + jnp.sum((first + second) * wt[j], axis=1, keepdims=True)
        packed = polarity.astype(jnp.bfloat16)
        sgn[j] = packed
        for part in range(3):
            sign3[j, part * sp : (part + 1) * sp, :] = packed

    def split_out(value):
        for j in range(n):
            top, left = (j // (dp // LANES)) * cr, (j % (dp // LANES)) * LANES
            stage[j] = value[top : top + cr, left : left + LANES]

    def scatter_start(phase_id, dst):
        def one(k, c):
            to = peer(k)
            pltpu.make_async_remote_copy(
                src_ref=stage.at[to], dst_ref=dst.at[me],
                send_sem=send_sem.at[phase_id, k], recv_sem=recv_sem.at[phase_id, me],
                device_id={"chan": to, "slot": slot}, device_id_type=pl.DeviceIdType.MESH,
            ).start()
            return c

        lax.fori_loop(1, n, one, 0)

    def gather_start(phase_id, dst):
        def one(k, c):
            pltpu.make_async_remote_copy(
                src_ref=dst.at[me], dst_ref=dst.at[me],
                send_sem=send_sem.at[phase_id, k], recv_sem=recv_sem.at[phase_id, me],
                device_id={"chan": peer(k), "slot": slot},
                device_id_type=pl.DeviceIdType.MESH,
            ).start()
            return c

        lax.fori_loop(1, n, one, 0)

    def finish(phase_id, dst):
        def one(k, c):
            src = peer(k)
            pltpu.make_async_remote_copy(
                src_ref=dst.at[src], dst_ref=dst.at[src],
                send_sem=send_sem.at[phase_id, k], recv_sem=recv_sem.at[phase_id, src],
                device_id={"chan": src, "slot": slot}, device_id_type=pl.DeviceIdType.MESH,
            ).wait()
            return c

        lax.fori_loop(1, n, one, 0)

    def total(buf):
        value = buf[0]
        for j in range(1, n):
            value = value + buf[j]
        return value

    def join(buf, out):
        for j in range(n):
            top, left = (j // (dp // LANES)) * cr, (j % (dp // LANES)) * LANES
            out[top : top + cr, left : left + LANES] = buf[j]

    tec[...] = jnp.zeros((sp, dp), jnp.float32)
    tec[0 : tec0_ref.shape[1], 0:srcs] = tec0_ref[0]
    acc[...] = jnp.zeros((sp, dp), jnp.float32)
    acc[0:1, 0:srcs] = flux_ref[...]
    flux_row = acc[0:1, :]
    part_den = (weight_sum * (scale * scale)) * (flux_row * flux_row)
    for j in range(n):
        top, left = (j // (dp // LANES)) * cr, (j % (dp // LANES)) * LANES
        fbuf[j] = tec[top : top + cr, left : left + LANES]
    split_out(part_den)
    ebuf[me] = stage[me]

    pl.semaphore_wait(barrier, (n - 1) + n * len(offs))
    scatter_start(4, ebuf)

    for j in range(tiles):
        coords = bv_ref[0][:, j * TILE : min((j + 1) * TILE, base_n)]
        width = coords.shape[1]
        value = (
            cols_ref[:, 1:2] * coords[0:1, :]
            + cols_ref[:, 2:3] * coords[1:2, :]
            + cols_ref[:, 3:4] * coords[2:3, :]
        ) * freq
        if width < TILE:
            geom[j] = jnp.zeros((drows, TILE), jnp.float32)
        geom[j, :, 0:width] = value

    lane_s = lax.broadcasted_iota(jnp.int32, (rpad, sp), 1)
    hot_s = (smap_ref[...] == lane_s).astype(jnp.float32)
    for part in range(3):
        ones3[:, part * sp : (part + 1) * sp] = hot_s.astype(jnp.bfloat16)
    lane_d = lax.broadcasted_iota(jnp.int32, (rpad, dp), 1)
    hot_d = (dmap_ref[...] == lane_d).astype(jnp.float32)
    onedf[...] = hot_d
    oned[...] = hot_d.astype(jnp.bfloat16)

    finish(4, ebuf)
    den_sum = total(ebuf)
    den[...] = jnp.where(den_sum == 0.0, 1.0, den_sum)
    load.wait()

    last = slots - 1
    neighbours = jnp.where(slot > 0, 1.0, 0.0) + jnp.where(slot < last, 1.0, 0.0)

    def iteration(it, carry):
        par = lax.rem(it, 2)
        join(fbuf, tec)
        turned = (tec[...] * turn_scale).T
        for part, piece in enumerate(split3(turned)):
            tec3[:, part * sp : (part + 1) * sp] = piece
        acc[...] = jnp.zeros((sp, dp), jnp.float32)

        def pair_tile(j, c):
            phase[...] = dot32(tec3[0:drows, :], sign3[j], 1, 0) + geom[j]
            sum_re = jnp.zeros((8, TILE), jnp.float32)
            sum_im = jnp.zeros((8, TILE), jnp.float32)
            for top in range(0, drows, 16):
                t = phase[top : top + 16, :]
                r = t - jnp.round(t)
                u = r * r
                flux = fluxb[top : top + 16, :]
                re = horner(COS_TERMS, u) * flux
                im = horner(SIN_TERMS, u) * (r * flux)
                mre[top : top + 16, :] = re
                mim[top : top + 16, :] = im
                sum_re = sum_re + re[0:8] + re[8:16]
                sum_im = sum_im + im[0:8] + im[8:16]
            left_re = visr[j] - jnp.sum(sum_re, axis=0, keepdims=True)
            left_im = visi[j] - jnp.sum(sum_im, axis=0, keepdims=True)
            rr_out[j] = left_re
            ri_out[j] = left_im
            wre = wt[j] * left_re
            wim = wt[j] * left_im
            for top in range(0, drows, 16):
                p = mre[top : top + 16, :] * wim - mim[top : top + 16, :] * wre
                hi = p.astype(jnp.bfloat16)
                phi[top : top + 16, :] = hi
                plo[top : top + 16, :] = (p - hi.astype(jnp.float32)).astype(jnp.bfloat16)
            acc[:, 0:drows] += dot32(sgn[j], phi[...], 1, 1) + dot32(sgn[j], plo[...], 1, 1)
            return c

        lax.fori_loop(0, tiles, pair_tile, 0)

        split_out(acc[...] * scale)
        abuf[me] = stage[me]
        scatter_start(0, abuf)
        finish(0, abuf)
        bbuf[me] = fbuf[me] + total(abuf) / den[...]
        gather_start(1, bbuf)
        finish(1, bbuf)
        join(bbuf, acc)

        field = jnp.concatenate([x for x in split3(acc[...])], axis=0)
        picked = dot32(ones3[...], field, 1, 0) * onedf[...]
        target[...] = jnp.broadcast_to(jnp.sum(picked, axis=1, keepdims=True), (rpad, LANES))

        def raw_step(i, sums):
            at = pl.ds(pl.multiple_of(i * 8, 8), 8)
            t = target[at, :]
            return tuple(
                s + basis[at, q * LANES : (q + 1) * LANES] * t for q, s in enumerate(sums)
            )

        zero = jnp.zeros((8, LANES), jnp.float32)
        sums = lax.fori_loop(0, rows // 8, raw_step, tuple(zero for _ in range(kk // LANES)))
        row = jnp.concatenate([jnp.sum(s, axis=0, keepdims=True) for s in sums], axis=1)
        if whole8 < rows:
            rest = target[whole8:rows, 0:1] * basis[whole8:rows, :]
            row = row + jnp.sum(rest, axis=0, keepdims=True)
        row = row * ew_ref[...]
        for j in range(n):
            craw[j] = row[:, j * cw : (j + 1) * cw]
        cbuf[par, 0, me] = craw[me]

        def c_copy(g, off, k):
            to = peer(k)
            return pltpu.make_async_remote_copy(
                src_ref=craw.at[to], dst_ref=cbuf.at[par, g, me],
                send_sem=csend.at[g, k], recv_sem=crecv.at[par, g, me],
                device_id={"chan": to, "slot": lax.rem(slot + off, slots)},
                device_id_type=pl.DeviceIdType.MESH,
            )

        def c_wait(g, off, k):
            src = peer(k)
            pltpu.make_async_remote_copy(
                src_ref=craw.at[src], dst_ref=cbuf.at[par, g, src],
                send_sem=csend.at[g, k], recv_sem=crecv.at[par, g, src],
                device_id={"chan": src, "slot": lax.rem(slot + off, slots)},
                device_id_type=pl.DeviceIdType.MESH,
            ).wait()

        groups = [0] + offs
        for g, off in enumerate(groups):

            def start_one(k, c, g=g, off=off):
                c_copy(g, off, k).start()
                return c

            lax.fori_loop(1 if off == 0 else 0, n, start_one, 0)
        for g, off in enumerate(groups):

            def wait_one(k, c, g=g, off=off):
                c_wait(g, off, k)
                return c

            lax.fori_loop(1 if off == 0 else 0, n, wait_one, 0)
        smooth = total(cbuf.at[par, 0])
        for g, off in enumerate(groups):
            if off:
                source = lax.rem(slot - off + slots, slots)
                near = jnp.abs(source - slot) == 1
                smooth = smooth + total(cbuf.at[par, g]) * jnp.where(near, SMOOTHING, 0.0)
        dbuf[me] = smooth / (1.0 + SMOOTHING * neighbours)
        gather_start(2, dbuf)
        finish(2, dbuf)
        coef = jnp.concatenate([dbuf[j] for j in range(n)], axis=1)
        coef_out[...] = coef
        wide = [
            jnp.broadcast_to(coef[:, q * LANES : (q + 1) * LANES], (8, LANES))
            for q in range(kk // LANES)
        ]

        def screen_step(i, c):
            at = pl.ds(pl.multiple_of(i * 8, 8), 8)
            value = basis[at, 0:LANES] * wide[0]
            for q in range(1, kk // LANES):
                value = value + basis[at, q * LANES : (q + 1) * LANES] * wide[q]
            target[at, :] = value
            return c

        lax.fori_loop(0, rows // 8, screen_step, 0)
        if whole8 < rows:
            value = basis[whole8:rows, 0:LANES] * wide[0][0 : rows - whole8]
            for q in range(1, kk // LANES):
                value = value + (
                    basis[whole8:rows, q * LANES : (q + 1) * LANES] * wide[q][0 : rows - whole8]
                )
            target[whole8:rows, :] = value
        screen = jnp.sum(target[...], axis=1, keepdims=True)
        hot = ones3[:, 0:sp].astype(jnp.float32)
        for part, piece in enumerate(split3(screen)):
            place[:, part * sp : (part + 1) * sp] = (
                hot * piece.astype(jnp.float32)
            ).astype(jnp.bfloat16)
        placed = dot32(place[...], oned[...], 0, 0)
        split_out(placed[0:sp] + placed[sp : 2 * sp] + placed[2 * sp : 3 * sp])
        ebuf[me] = stage[me]
        scatter_start(4, ebuf)
        finish(4, ebuf)
        fbuf[me] = total(ebuf)
        gather_start(3, fbuf)
        finish(3, fbuf)
        return carry

    lax.fori_loop(0, ITERS, iteration, 0)
    join(fbuf, tec)
    tec_out[0] = tec[0 : tec0_ref.shape[1], 0:srcs]


def per_device(
    n, slots,
    measured_real, measured_imaginary, measured_weight, baseline_vectors, antenna_pairs,
    directions, direction_flux, channel_frequency, electron_content_start,
    pierce_station_direction, eigen_basis, eigen_weight,
):
    shard_slots, shard_channels, base_n = measured_real.shape
    assert shard_slots == 1 and shard_channels == 1
    stations, srcs = electron_content_start.shape[1:]
    rows, kk = eigen_basis.shape
    tiles = -(-base_n // TILE)
    drows = round_up(srcs, 16)
    dp = round_up(srcs, LANES)
    sp = round_up(stations, 64)
    cr = sp * (dp // LANES) // n
    rpad = round_up(rows + 1, 16)
    cw = kk // n
    assert cr * n == sp * (dp // LANES) and cw * n == kk and kk % LANES == 0
    groups = 1 + len({1 % slots, (slots - 1) % slots} - {0})

    own = lax.dynamic_slice_in_dim(
        pierce_station_direction[0], lax.axis_index("chan") * rows, rows, 0
    )
    own = jnp.pad(own, (0, rpad - rows), constant_values=-1)[:, None]
    smap = jnp.where(own < 0, -1, own // srcs)
    dmap = jnp.where(own < 0, -1, own % srcs)
    pairs = jnp.pad(antenna_pairs, ((0, 0), (0, tiles * TILE - base_n)), constant_values=-1)
    cols = jnp.pad(
        jnp.concatenate([direction_flux, directions], axis=0).T, ((0, drows - srcs), (0, 0))
    )
    f32, bf16 = jnp.float32, jnp.bfloat16
    vmem = pl.BlockSpec(memory_space=pltpu.VMEM)
    geo = (n, slots, tiles, base_n, srcs, drows, sp, dp, cr, rows, rpad, kk, cw)
    tec_final, coefficients, res_re, res_im = pl.pallas_call(
        functools.partial(solve_kernel, geo),
        out_shape=(
            jax.ShapeDtypeStruct((1, stations, srcs), f32),
            jax.ShapeDtypeStruct((1, kk), f32),
            jax.ShapeDtypeStruct((tiles, 1, TILE), f32),
            jax.ShapeDtypeStruct((tiles, 1, TILE), f32),
        ),
        in_specs=[vmem] * 11 + [pl.BlockSpec(memory_space=pl.ANY)] + [vmem],
        out_specs=(vmem,) * 4,
        scratch_shapes=[
            pltpu.VMEM((tiles, 1, TILE), f32),
            pltpu.VMEM((tiles, 1, TILE), f32),
            pltpu.VMEM((tiles, 1, TILE), f32),
            pltpu.VMEM((tiles, drows, TILE), f32),
            pltpu.VMEM((tiles, 3 * sp, TILE), bf16),
            pltpu.VMEM((tiles, sp, TILE), bf16),
            pltpu.VMEM((drows, TILE), f32),
            pltpu.VMEM((drows, TILE), f32),
            pltpu.VMEM((drows, TILE), f32),
            pltpu.VMEM((drows, TILE), f32),
            pltpu.VMEM((drows, TILE), bf16),
            pltpu.VMEM((drows, TILE), bf16),
            pltpu.VMEM((sp, dp), f32),
            pltpu.VMEM((dp, 3 * sp), bf16),
            pltpu.VMEM((sp, dp), f32),
            pltpu.VMEM((cr, LANES), f32),
            pltpu.VMEM((rows, kk), f32),
            pltpu.VMEM((rpad, 3 * sp), bf16),
            pltpu.VMEM((rpad, dp), bf16),
            pltpu.VMEM((rpad, dp), f32),
            pltpu.VMEM((rpad, LANES), f32),
            pltpu.VMEM((rpad, 3 * sp), bf16),
            pltpu.VMEM((n, cr, LANES), f32),
            pltpu.VMEM((n, cr, LANES), f32),
            pltpu.VMEM((n, cr, LANES), f32),
            pltpu.VMEM((n, 1, cw), f32),
            pltpu.VMEM((2, groups, n, 1, cw), f32),
            pltpu.VMEM((n, 1, cw), f32),
            pltpu.VMEM((n, cr, LANES), f32),
            pltpu.VMEM((n, cr, LANES), f32),
            pltpu.SemaphoreType.DMA,
            pltpu.SemaphoreType.DMA((5, n)),
            pltpu.SemaphoreType.DMA((5, n)),
            pltpu.SemaphoreType.DMA((groups, n)),
            pltpu.SemaphoreType.DMA((2, groups, n)),
        ],
        compiler_params=pltpu.CompilerParams(
            collective_id=0, has_side_effects=True, vmem_limit_bytes=60 * 1024 * 1024
        ),
    )(
        measured_real, measured_imaginary, measured_weight, baseline_vectors, pairs, cols,
        direction_flux, channel_frequency.reshape(1, 1), electron_content_start,
        smap, dmap, eigen_basis, eigen_weight.reshape(1, kk),
    )
    res_re = res_re.reshape(1, 1, tiles * TILE)[:, :, :base_n]
    res_im = res_im.reshape(1, 1, tiles * TILE)[:, :, :base_n]
    return tec_final, coefficients, res_re, res_im


def solution(mesh):
    in_specs = (
        P("slot", "chan", None),
        P("slot", "chan", None),
        P("slot", "chan", None),
        P("slot", None, None),
        P(),
        P(),
        P("chan", None),
        P("chan"),
        P("slot", None, None),
        P("slot", None),
        P("chan", None),
        P(),
    )
    out_specs = (
        P("slot", None, None),
        P("slot", None),
        P("slot", "chan", None),
        P("slot", "chan", None),
    )
    body = functools.partial(per_device, mesh.shape["chan"], mesh.shape["slot"])
    return jax.shard_map(body, mesh=mesh, in_specs=in_specs, out_specs=out_specs, check_vma=False)
```

time: 794 us -> 168 us (0.21); the launches traced: 785 us -> 167 us
  blocking collectives: 526 us -> 0 us
  Pallas kernels: 0 us -> 153 us
  matrix products: 112 us -> 0 us
  waiting for transfers between devices: 95.7 us -> 0 us
  starting transfers between devices: 23.4 us -> 0 us
  between operations: 15.8 us -> 1.33 us
    psum x11 -> x0, blocking collectives: 526 us -> none  [the longest x4 232 us: per_device(): tec_flat = lax.psum(placed, 'chan')]
    pallas_call x0 -> x1, Pallas kernels: none -> 153 us  [per_device(): pl.pallas_call(functools.partial(solve_kernel, geo), out_shape=(jax.Shape...]
    dot_general x26 -> x0, matrix products: 112 us -> none  [the longest x4 28.3 us: per_device(): screen_own = jnp.dot(smooth, eigen_basis.T, precision=HIGHEST)]
    psum x1 -> x0, waiting for transfers between devices: 90.9 us -> none  [reduce_normals(): return lax.psum(values, 'chan')]
    ppermute x8 -> x0, starting transfers between devices: 23.3 us -> none  [the longest x4 18.2 us: padded_2(): lax.ppermute(tail, axis, [(i, (i + 1) % count) for i in range(ends)])]
  transfers between devices with their start and end apart: 9 -> 0, of which waited for: 5 -> 0; matrix products, arithmetic and copies ran while one was open for 0% -> 0% of each run, Pallas kernels for 0% -> 0%
where the time goes in v1:
time: 168 us; the launch traced here: 167 us
  Pallas kernels  153 us (91%)
  local copies, waits for them, and re-layouts  12.3 us (7%)
    pallas_call x1, Pallas kernels, per_device(): pl.pallas_call(functools.partial(solve_kernel, geo), out_shape=(jax.Shape...  153 us
    unnamed x8, local copies, waits for them, and re-layouts  8.35 us

profile of v1, /device:TPU:0, one launch (start us, length us, event | category | flops | bytes accessed | tf_op | source)
XLA Modules:
  0.0 167.2 jit_solution(4395041361882468635)
XLA Ops:
  0.6 0.0 copy-start
  1.3 0.1 copy-done
  1.4 0.1 dynamic-slice_reduce_fusion
  1.5 0.7 pad_maximum_fusion
  2.3 1.3 pad.12.pairs_ref
  3.6 1.3 copy.29.bv_ref
  4.9 1.5 copy.30.tec0_ref
  6.4 0.1 copy.28
  6.5 0.7 pad.13.cols_ref
  7.2 0.9 select_n.36.dmap_ref
  8.1 0.9 select_n.35.smap_ref
  9.0 152.8 %shard_map.147 = (f32[1,60,200]{2,1,0:T(8,128)}, f32[1,2048]{1,0:T(1,128)}, f32[7,1,256]{2,1,0:T(1,128)}, f32[7,1,256]{2,1,0:T(1,128)}) custom-call(f32[1,1,1770]{2,1,0:T(1,128)} %vr_ref.1, f32[1,1,1770]{2,1,0:T(1,128)} %vi_ref.1, f32[1,1,1770]{2,1,0:T(1,128)} %w_ref.1, f32[1,3,1770]{2,1,0:T(4,128)} %copy.29.bv_ref, s32[2,1792]{1,0:T(2,128)} %pad.12.pairs_ref, ...), custom_call_target="tpu_custom_call" | custom-call | tf_op jit(solution)/shard_map/pallas_call | solution.py:414
  161.8 1.5 copy.33
  163.3 1.3 copy.38
  164.6 1.3 copy.39
  165.9 1.3 copy.40
  (1 shorter events, 0.0 us)
Async XLA Ops:
  0.6 0.8 copy-start

commit v2 on v1

--- a/solution.py
+++ b/solution.py
@@ -61,10 +61,10 @@
 
 def solve_kernel(
     geo,
-    vr_ref, vi_ref, w_ref, bv_ref, pairs_ref, cols_ref, flux_ref, freq_ref, tec0_ref,
-    smap_ref, dmap_ref, basis_ref, ew_ref,
+    vr_ref, vi_ref, w_ref, bv_ref, pairs_ref, dir_ref, flux_ref, freq_ref, tec0_ref,
+    own_ref, basis_ref, ew_ref,
     tec_out, coef_out, rr_out, ri_out,
-    visr, visi, wt, geom, sign3, sgn, fluxb, phase, mre, mim, phi, plo,
+    resr, resi, cols, mapt, visr, visi, wt, geom, sign3, sgn, fluxb, phase, mre, mim, phi, plo,
     tec, tec3, acc, den, basis, ones3, oned, onedf, target, place,
     stage, abuf, bbuf, craw, cbuf, dbuf, ebuf, fbuf,
     basis_sem, send_sem, recv_sem, csend, crecv,
@@ -77,6 +77,23 @@
     def peer(k):
         return lax.rem(me + k, n)
 
+    bits = n.bit_length() - 1
+    if n == 1 << bits:
+        flips = []
+        rest = me
+        for b in range(bits):
+            flips.append((1 - 2 * lax.rem(rest, 2)) * (1 << b))
+            rest = rest // 2
+
+        def partner(k):
+            to = me
+            for b in range(bits):
+                if (k >> b) & 1:
+                    to = to + flips[b]
+            return to
+    else:
+        partner = peer
+
     whole8 = rows // 8 * 8
     load = pltpu.make_async_copy(basis_ref, basis, basis_sem)
     load.start()
@@ -103,66 +120,84 @@
 
         lax.fori_loop(0, n, greet_far, 0)
 
-    freq = freq_ref[...]
+    freq = jnp.full((1, 1), freq_ref[0], jnp.float32)
     scale = TEC_PHASE / freq
     turn_scale = (TEC_PHASE / TWO_PI) / freq
-    fluxb[...] = jnp.broadcast_to(cols_ref[:, 0:1], (drows, TILE))
-    station = lax.broadcasted_iota(jnp.int32, (sp, TILE), 0)
+    acc[...] = jnp.zeros((sp, dp), jnp.float32)
+    acc[0:1, 0:srcs] = flux_ref[...]
+    acc[1:4, 0:srcs] = dir_ref[...]
+    flux_row = acc[0:1, :]
+    cols[...] = acc[0:8, :].T
+    fluxb[...] = jnp.broadcast_to(cols[0:drows, 0:1], (drows, TILE))
     weight_sum = jnp.zeros((sp, 1), jnp.float32)
     for j in range(tiles):
         lo = j * TILE
         width = min(TILE, base_n - lo)
-        for dst, src in ((visr, vr_ref[0]), (visi, vi_ref[0]), (wt, w_ref[0])):
+        if width < TILE:
+            sgn[j] = jnp.zeros((sp, TILE), jnp.bfloat16)
+            sign3[j] = jnp.zeros((3 * sp, TILE), jnp.bfloat16)
+            geom[j] = jnp.zeros((drows, TILE), jnp.float32)
+        for dst, src in ((visr, vr_ref), (visi, vi_ref), (wt, w_ref)):
             if width < TILE:
                 dst[j] = jnp.zeros((1, TILE), jnp.float32)
-            dst[j, :, 0:width] = src[:, lo : lo + width]
-        pairs = pairs_ref[:, lo : lo + TILE]
-        first = (pairs[0:1, :] == station).astype(jnp.float32)
-        second = (pairs[1:2, :] == station).astype(jnp.float32)
-        polarity = first - second
-        weight_sum = weight_sum + jnp.sum((first + second) * wt[j], axis=1, keepdims=True)
-        packed = polarity.astype(jnp.bfloat16)
-        sgn[j] = packed
+            dst[j, :, 0:width] = src[0, :, lo : lo + width]
+        station = lax.broadcasted_iota(jnp.int32, (sp, width), 0)
+        first = (pairs_ref[0:1, lo : lo + width] == station).astype(jnp.float32)
+        second = (pairs_ref[1:2, lo : lo + width] == station).astype(jnp.float32)
+        weight_sum = weight_sum + jnp.sum(
+            (first + second) * w_ref[0, :, lo : lo + width], axis=1, keepdims=True
+        )
+        packed = (first - second).astype(jnp.bfloat16)
+        sgn[j, :, 0:width] = packed
         for part in range(3):
-            sign3[j, part * sp : (part + 1) * sp, :] = packed
+            sign3[j, part * sp : (part + 1) * sp, 0:width] = packed
+        geom[j, :, 0:width] = (
+            cols[0:drows, 1:2] * bv_ref[0, :, lo : lo + width]
+            + cols[0:drows, 2:3] * bv_ref[1, :, lo : lo + width]
+            + cols[0:drows, 3:4] * bv_ref[2, :, lo : lo + width]
+        ) * freq
 
     def split_out(value):
         for j in range(n):
             top, left = (j // (dp // LANES)) * cr, (j % (dp // LANES)) * LANES
             stage[j] = value[top : top + cr, left : left + LANES]
 
+    def copy_of(phase_id, src, dst, k, slot_of_src):
+        to = partner(k)
+        return pltpu.make_async_remote_copy(
+            src_ref=src.at[to if slot_of_src else me], dst_ref=dst.at[me],
+            send_sem=send_sem.at[phase_id, k], recv_sem=recv_sem.at[phase_id, me],
+            device_id={"chan": to, "slot": slot}, device_id_type=pl.DeviceIdType.MESH,
+        )
+
     def scatter_start(phase_id, dst):
+        for k in range(n - 1, 0, -1):
+            copy_of(phase_id, stage, dst, k, True).start()
+
+    def gather_start(phase_id, dst):
+        for k in range(n - 1, 0, -1):
+            copy_of(phase_id, dst, dst, k, False).start()
+
+    def receive(phase_id, dst):
         def one(k, c):
-            to = peer(k)
+            src = peer(k)
             pltpu.make_async_remote_copy(
-                src_ref=stage.at[to], dst_ref=dst.at[me],
-                send_sem=send_sem.at[phase_id, k], recv_sem=recv_sem.at[phase_id, me],
-                device_id={"chan": to, "slot": slot}, device_id_type=pl.DeviceIdType.MESH,
-            ).start()
+                src_ref=dst.at[src], dst_ref=dst.at[src],
+                send_sem=send_sem.at[phase_id, 0], recv_sem=recv_sem.at[phase_id, src],
+                device_id={"chan": src, "slot": slot}, device_id_type=pl.DeviceIdType.MESH,
+            ).wait_recv()
             return c
 
         lax.fori_loop(1, n, one, 0)
 
-    def gather_start(phase_id, dst):
+    def drain(phase_id, dst):
         def one(k, c):
             pltpu.make_async_remote_copy(
                 src_ref=dst.at[me], dst_ref=dst.at[me],
                 send_sem=send_sem.at[phase_id, k], recv_sem=recv_sem.at[phase_id, me],
                 device_id={"chan": peer(k), "slot": slot},
                 device_id_type=pl.DeviceIdType.MESH,
-            ).start()
-            return c
-
-        lax.fori_loop(1, n, one, 0)
-
-    def finish(phase_id, dst):
-        def one(k, c):
-            src = peer(k)
-            pltpu.make_async_remote_copy(
-                src_ref=dst.at[src], dst_ref=dst.at[src],
-                send_sem=send_sem.at[phase_id, k], recv_sem=recv_sem.at[phase_id, src],
-                device_id={"chan": src, "slot": slot}, device_id_type=pl.DeviceIdType.MESH,
-            ).wait()
+            ).wait_send()
             return c
 
         lax.fori_loop(1, n, one, 0)
@@ -179,10 +214,8 @@
             out[top : top + cr, left : left + LANES] = buf[j]
 
     tec[...] = jnp.zeros((sp, dp), jnp.float32)
-    tec[0 : tec0_ref.shape[1], 0:srcs] = tec0_ref[0]
-    acc[...] = jnp.zeros((sp, dp), jnp.float32)
-    acc[0:1, 0:srcs] = flux_ref[...]
-    flux_row = acc[0:1, :]
+    for st in range(tec0_ref.shape[0]):
+        tec[st : st + 1, 0:srcs] = tec0_ref[st]
     part_den = (weight_sum * (scale * scale)) * (flux_row * flux_row)
     for j in range(n):
         top, left = (j // (dp // LANES)) * cr, (j % (dp // LANES)) * LANES
@@ -190,34 +223,22 @@
     split_out(part_den)
     ebuf[me] = stage[me]
 
+    mapt[...] = jnp.full(mapt.shape, -1.0, jnp.float32)
+    mapt[:, 0:rows] = jnp.broadcast_to(own_ref[...].astype(jnp.float32), (8, rows))
+    place_col = mapt[...].T[0:rpad, 0:1]
+    station_col = jnp.floor((place_col + 0.5) * (1.0 / srcs))
+    direction_col = place_col - station_col * srcs
+    lane_s = lax.broadcasted_iota(jnp.int32, (rpad, sp), 1).astype(jnp.float32)
+    hot_s = (station_col == lane_s).astype(jnp.float32)
+    for part in range(3):
+        ones3[:, part * sp : (part + 1) * sp] = hot_s.astype(jnp.bfloat16)
+    lane_d = lax.broadcasted_iota(jnp.int32, (rpad, dp), 1).astype(jnp.float32)
+    hot_d = ((direction_col == lane_d) & (place_col >= 0.0)).astype(jnp.float32)
+    onedf[...] = hot_d
+    oned[...] = hot_d.astype(jnp.bfloat16)
+
     pl.semaphore_wait(barrier, (n - 1) + n * len(offs))
     scatter_start(4, ebuf)
-
-    for j in range(tiles):
-        coords = bv_ref[0][:, j * TILE : min((j + 1) * TILE, base_n)]
-        width = coords.shape[1]
-        value = (
-            cols_ref[:, 1:2] * coords[0:1, :]
-            + cols_ref[:, 2:3] * coords[1:2, :]
-            + cols_ref[:, 3:4] * coords[2:3, :]
-        ) * freq
-        if width < TILE:
-            geom[j] = jnp.zeros((drows, TILE), jnp.float32)
-        geom[j, :, 0:width] = value
-
-    lane_s = lax.broadcasted_iota(jnp.int32, (rpad, sp), 1)
-    hot_s = (smap_ref[...] == lane_s).astype(jnp.float32)
-    for part in range(3):
-        ones3[:, part * sp : (part + 1) * sp] = hot_s.astype(jnp.bfloat16)
-    lane_d = lax.broadcasted_iota(jnp.int32, (rpad, dp), 1)
-    hot_d = (dmap_ref[...] == lane_d).astype(jnp.float32)
-    onedf[...] = hot_d
-    oned[...] = hot_d.astype(jnp.bfloat16)
-
-    finish(4, ebuf)
-    den_sum = total(ebuf)
-    den[...] = jnp.where(den_sum == 0.0, 1.0, den_sum)
-    load.wait()
 
     last = slots - 1
     neighbours = jnp.where(slot > 0, 1.0, 0.0) + jnp.where(slot < last, 1.0, 0.0)
@@ -247,8 +268,8 @@
                 sum_im = sum_im + im[0:8] + im[8:16]
             left_re = visr[j] - jnp.sum(sum_re, axis=0, keepdims=True)
             left_im = visi[j] - jnp.sum(sum_im, axis=0, keepdims=True)
-            rr_out[j] = left_re
-            ri_out[j] = left_im
+            resr[j] = left_re
+            resi[j] = left_im
             wre = wt[j] * left_re
             wim = wt[j] * left_im
             for top in range(0, drows, 16):
@@ -261,13 +282,30 @@
 
         lax.fori_loop(0, tiles, pair_tile, 0)
 
+        @pl.when(it == 0)
+        def _():
+            drain(4, ebuf)
+
+        @pl.when(it > 0)
+        def _():
+            drain(3, fbuf)
+
         split_out(acc[...] * scale)
+        scatter_start(0, abuf)
         abuf[me] = stage[me]
-        scatter_start(0, abuf)
-        finish(0, abuf)
+
+        @pl.when(it == 0)
+        def _():
+            receive(4, ebuf)
+            den_sum = total(ebuf)
+            den[...] = jnp.where(den_sum == 0.0, 1.0, den_sum)
+            load.wait()
+
+        receive(0, abuf)
         bbuf[me] = fbuf[me] + total(abuf) / den[...]
         gather_start(1, bbuf)
-        finish(1, bbuf)
+        drain(0, abuf)
+        receive(1, bbuf)
         join(bbuf, acc)
 
         field = jnp.concatenate([x for x in split3(acc[...])], axis=0)
@@ -292,36 +330,24 @@
             craw[j] = row[:, j * cw : (j + 1) * cw]
         cbuf[par, 0, me] = craw[me]
 
-        def c_copy(g, off, k):
-            to = peer(k)
+        def c_copy(g, off, to, src, k):
             return pltpu.make_async_remote_copy(
-                src_ref=craw.at[to], dst_ref=cbuf.at[par, g, me],
-                send_sem=csend.at[g, k], recv_sem=crecv.at[par, g, me],
+                src_ref=craw.at[to], dst_ref=cbuf.at[par, g, src],
+                send_sem=csend.at[g, k], recv_sem=crecv.at[par, g, src],
                 device_id={"chan": to, "slot": lax.rem(slot + off, slots)},
                 device_id_type=pl.DeviceIdType.MESH,
             )
 
-        def c_wait(g, off, k):
-            src = peer(k)
-            pltpu.make_async_remote_copy(
-                src_ref=craw.at[src], dst_ref=cbuf.at[par, g, src],
-                send_sem=csend.at[g, k], recv_sem=crecv.at[par, g, src],
-                device_id={"chan": src, "slot": lax.rem(slot + off, slots)},
-                device_id_type=pl.DeviceIdType.MESH,
-            ).wait()
-
         groups = [0] + offs
+        for k in range(n - 1, -1, -1):
+            for g, off in reversed(list(enumerate(groups))):
+                if k or off:
+                    c_copy(g, off, partner(k), me, k).start()
+        drain(1, bbuf)
         for g, off in enumerate(groups):
 
-            def start_one(k, c, g=g, off=off):
-                c_copy(g, off, k).start()
-                return c
-
-            lax.fori_loop(1 if off == 0 else 0, n, start_one, 0)
-        for g, off in enumerate(groups):
-
             def wait_one(k, c, g=g, off=off):
-                c_wait(g, off, k)
+                c_copy(g, off, peer(k), peer(k), k).wait_recv()
                 return c
 
             lax.fori_loop(1 if off == 0 else 0, n, wait_one, 0)
@@ -333,7 +359,14 @@
                 smooth = smooth + total(cbuf.at[par, g]) * jnp.where(near, SMOOTHING, 0.0)
         dbuf[me] = smooth / (1.0 + SMOOTHING * neighbours)
         gather_start(2, dbuf)
-        finish(2, dbuf)
+        for g, off in enumerate(groups):
+
+            def drain_one(k, c, g=g, off=off):
+                c_copy(g, off, peer(k), peer(k), k).wait_send()
+                return c
+
+            lax.fori_loop(1 if off == 0 else 0, n, drain_one, 0)
+        receive(2, dbuf)
         coef = jnp.concatenate([dbuf[j] for j in range(n)], axis=1)
         coef_out[...] = coef
         wide = [
@@ -365,17 +398,26 @@
             ).astype(jnp.bfloat16)
         placed = dot32(place[...], oned[...], 0, 0)
         split_out(placed[0:sp] + placed[sp : 2 * sp] + placed[2 * sp : 3 * sp])
+        scatter_start(4, ebuf)
         ebuf[me] = stage[me]
-        scatter_start(4, ebuf)
-        finish(4, ebuf)
+        drain(2, dbuf)
+        receive(4, ebuf)
         fbuf[me] = total(ebuf)
         gather_start(3, fbuf)
-        finish(3, fbuf)
+        drain(4, ebuf)
+        receive(3, fbuf)
         return carry
 
     lax.fori_loop(0, ITERS, iteration, 0)
+    drain(3, fbuf)
     join(fbuf, tec)
-    tec_out[0] = tec[0 : tec0_ref.shape[1], 0:srcs]
+    for st in range(tec0_ref.shape[0]):
+        tec_out[st] = tec[st : st + 1, 0:srcs]
+    for j in range(tiles):
+        lo = j * TILE
+        width = min(TILE, base_n - lo)
+        rr_out[0, :, lo : lo + width] = resr[j, :, 0:width]
+        ri_out[0, :, lo : lo + width] = resi[j, :, 0:width]
 
 
 def per_device(
@@ -401,27 +443,28 @@
     own = lax.dynamic_slice_in_dim(
         pierce_station_direction[0], lax.axis_index("chan") * rows, rows, 0
     )
-    own = jnp.pad(own, (0, rpad - rows), constant_values=-1)[:, None]
-    smap = jnp.where(own < 0, -1, own // srcs)
-    dmap = jnp.where(own < 0, -1, own % srcs)
-    pairs = jnp.pad(antenna_pairs, ((0, 0), (0, tiles * TILE - base_n)), constant_values=-1)
-    cols = jnp.pad(
-        jnp.concatenate([direction_flux, directions], axis=0).T, ((0, drows - srcs), (0, 0))
-    )
     f32, bf16 = jnp.float32, jnp.bfloat16
     vmem = pl.BlockSpec(memory_space=pltpu.VMEM)
     geo = (n, slots, tiles, base_n, srcs, drows, sp, dp, cr, rows, rpad, kk, cw)
     tec_final, coefficients, res_re, res_im = pl.pallas_call(
         functools.partial(solve_kernel, geo),
         out_shape=(
-            jax.ShapeDtypeStruct((1, stations, srcs), f32),
+            jax.ShapeDtypeStruct((stations, 1, srcs), f32),
             jax.ShapeDtypeStruct((1, kk), f32),
-            jax.ShapeDtypeStruct((tiles, 1, TILE), f32),
-            jax.ShapeDtypeStruct((tiles, 1, TILE), f32),
+            jax.ShapeDtypeStruct((1, 1, base_n), f32),
+            jax.ShapeDtypeStruct((1, 1, base_n), f32),
         ),
-        in_specs=[vmem] * 11 + [pl.BlockSpec(memory_space=pl.ANY)] + [vmem],
+        in_specs=[vmem] * 7
+        + [pl.BlockSpec(memory_space=pltpu.SMEM)]
+        + [vmem] * 2
+        + [pl.BlockSpec(memory_space=pl.ANY)]
+        + [vmem],
         out_specs=(vmem,) * 4,
         scratch_shapes=[
+            pltpu.VMEM((tiles, 1, TILE), f32),
+            pltpu.VMEM((tiles, 1, TILE), f32),
+            pltpu.VMEM((dp, 8), f32),
+            pltpu.VMEM((8, round_up(rpad, LANES)), f32),
             pltpu.VMEM((tiles, 1, TILE), f32),
             pltpu.VMEM((tiles, 1, TILE), f32),
             pltpu.VMEM((tiles, 1, TILE), f32),
@@ -462,13 +505,12 @@
             collective_id=0, has_side_effects=True, vmem_limit_bytes=60 * 1024 * 1024
         ),
     )(
-        measured_real, measured_imaginary, measured_weight, baseline_vectors, pairs, cols,
-        direction_flux, channel_frequency.reshape(1, 1), electron_content_start,
-        smap, dmap, eigen_basis, eigen_weight.reshape(1, kk),
+        measured_real, measured_imaginary, measured_weight,
+        baseline_vectors.reshape(3, 1, base_n), antenna_pairs, directions,
+        direction_flux, channel_frequency, electron_content_start.reshape(stations, 1, srcs),
+        own.reshape(1, rows), eigen_basis, eigen_weight.reshape(1, kk),
     )
-    res_re = res_re.reshape(1, 1, tiles * TILE)[:, :, :base_n]
-    res_im = res_im.reshape(1, 1, tiles * TILE)[:, :, :base_n]
-    return tec_final, coefficients, res_re, res_im
+    return tec_final.reshape(1, stations, srcs), coefficients, res_re, res_im
 
 
 def solution(mesh):

time: 168 us -> 152 us (0.905)
  Pallas kernels: 153 us -> 144 us
  local copies, waits for them, and re-layouts: 12.3 us -> 6.13 us
    pallas_call x1, Pallas kernels: 153 us -> 144 us  [per_device(): pl.pallas_call(functools.partial(solve_kernel, geo), out_shape=(jax.Shape...]
    unnamed x8 -> x6, local copies, waits for them, and re-layouts: 8.35 us -> 5.48 us
    pad x2 -> x0, local copies, waits for them, and re-layouts: 1.98 us -> none  [the longest x1 1.32 us: per_device(): jnp.pad(antenna_pairs, ((0, 0), (0, tiles * TILE - base_n)), constant_val...]
    select_n x2 -> x0, local copies, waits for them, and re-layouts: 1.8 us -> none  [the longest x1 0.91 us: per_device(): dmap = jnp.where(own < 0, -1, own % srcs)]
where the time goes in v2:
time: 152 us; the launch traced here: 151 us
  Pallas kernels  144 us (95%)
  local copies, waits for them, and re-layouts  6.13 us (4%)
    pallas_call x1, Pallas kernels, per_device(): pl.pallas_call(functools.partial(solve_kernel, geo), out_shape=(jax.Shape...  144 us
    unnamed x6, local copies, waits for them, and re-layouts  5.48 us

profile of v2, /device:TPU:0, one launch (start us, length us, event | category | flops | bytes accessed | tf_op | source)
XLA Modules:
  0.0 151.4 jit_solution(15961975840137562825)
XLA Ops:
  0.6 0.0 copy-start
  1.3 0.1 copy-done
  1.4 0.7 constant_dynamic-slice_fusion.own_ref
  2.1 143.9 %shard_map.147 = (f32[60,1,200]{2,1,0:T(1,128)}, f32[1,2048]{1,0:T(1,128)}, f32[1,1,1770]{2,1,0:T(1,128)}, f32[1,1,1770]{2,1,0:T(1,128)}) custom-call(f32[1,1,1770]{2,1,0:T(1,128)} %vr_ref.1, f32[1,1,1770]{2,1,0:T(1,128)} %vi_ref.1, f32[1,1,1770]{2,1,0:T(1,128)} %w_ref.1, f32[3,1,1770]{2,1,0:T(1,128)} %bitcast.6, s32[2,1770]{1,0:T(2,128)} %pairs_ref.1, ...), custom_call_target="tpu_custom_call" | custom-call | tf_op jit(solution)/shard_map/pallas_call | solution.py:449
  146.1 1.5 copy.21
  147.5 1.3 copy.22
  148.8 1.3 copy.23
  150.1 1.3 copy.24
Async XLA Ops:
  0.6 0.8 copy-start

commit v3 on v2

--- a/solution.py
+++ b/solution.py
@@ -27,7 +27,7 @@
     r = np.sqrt(u)
     out = []
     for values in (np.cos(2 * np.pi * r), np.sin(2 * np.pi * r) / r):
-        cheb = np.polynomial.chebyshev.Chebyshev.fit(u, values, 7, domain=[0.0, 0.25])
+        cheb = np.polynomial.chebyshev.Chebyshev.fit(u, values, 6, domain=[0.0, 0.25])
         coefs = cheb.convert(kind=np.polynomial.Polynomial).coef
         out.append(tuple(float(np.float32(c)) for c in coefs))
     return out
@@ -67,9 +67,9 @@
     resr, resi, cols, mapt, visr, visi, wt, geom, sign3, sgn, fluxb, phase, mre, mim, phi, plo,
     tec, tec3, acc, den, basis, ones3, oned, onedf, target, place,
     stage, abuf, bbuf, craw, cbuf, dbuf, ebuf, fbuf,
-    basis_sem, send_sem, recv_sem, csend, crecv,
+    psum_in, basis_sem, send_sem, recv_sem, csend, crecv, swap_send, swap_recv,
 ):
-    n, slots, tiles, base_n, srcs, drows, sp, dp, cr, rows, rpad, kk, cw = geo
+    n, slots, tiles, base_n, srcs, drows, sp, dp, cr, rows, rpad, kk = geo
     me = lax.axis_index("chan")
     slot = lax.axis_index("slot")
     offs = sorted({1 % slots, (slots - 1) % slots} - {0})
@@ -95,6 +95,7 @@
         partner = peer
 
     whole8 = rows // 8 * 8
+    burst = max(f for f in (1, 2, 3) if (rows // 8) % f == 0)
     load = pltpu.make_async_copy(basis_ref, basis, basis_sem)
     load.start()
 
@@ -240,6 +241,18 @@
     pl.semaphore_wait(barrier, (n - 1) + n * len(offs))
     scatter_start(4, ebuf)
 
+    core = lax.rem(me, 2)
+    chip = me // 2
+    chips, half = n // 2, kk // 2
+
+    def swap(which, src, dst):
+        return pltpu.make_async_remote_copy(
+            src_ref=src, dst_ref=dst,
+            send_sem=swap_send.at[which], recv_sem=swap_recv.at[which],
+            device_id={"chan": me + 1 - 2 * core, "slot": slot},
+            device_id_type=pl.DeviceIdType.MESH,
+        )
+
     last = slots - 1
     neighbours = jnp.where(slot > 0, 1.0, 0.0) + jnp.where(slot < last, 1.0, 0.0)
 
@@ -313,61 +326,70 @@
         target[...] = jnp.broadcast_to(jnp.sum(picked, axis=1, keepdims=True), (rpad, LANES))
 
         def raw_step(i, sums):
-            at = pl.ds(pl.multiple_of(i * 8, 8), 8)
-            t = target[at, :]
-            return tuple(
-                s + basis[at, q * LANES : (q + 1) * LANES] * t for q, s in enumerate(sums)
-            )
+            for part in range(burst):
+                at = pl.ds(pl.multiple_of((i * burst + part) * 8, 8), 8)
+                t = target[at, :]
+                sums = tuple(
+                    s + basis[at, q * LANES : (q + 1) * LANES] * t for q, s in enumerate(sums)
+                )
+            return sums
 
         zero = jnp.zeros((8, LANES), jnp.float32)
-        sums = lax.fori_loop(0, rows // 8, raw_step, tuple(zero for _ in range(kk // LANES)))
+        sums = lax.fori_loop(0, rows // 8 // burst, raw_step, tuple(zero for _ in range(kk // LANES)))
         row = jnp.concatenate([jnp.sum(s, axis=0, keepdims=True) for s in sums], axis=1)
         if whole8 < rows:
             rest = target[whole8:rows, 0:1] * basis[whole8:rows, :]
             row = row + jnp.sum(rest, axis=0, keepdims=True)
         row = row * ew_ref[...]
-        for j in range(n):
-            craw[j] = row[:, j * cw : (j + 1) * cw]
-        cbuf[par, 0, me] = craw[me]
+        for h in range(2):
+            for q in range(half // LANES):
+                lo = h * half + q * LANES
+                craw[h, q : q + 1, :] = row[:, lo : lo + LANES]
+        swap(0, craw.at[1 - core], psum_in.at[0]).start()
+        drain(1, bbuf)
+        swap(0, craw.at[1 - core], psum_in.at[0]).wait()
+        mine = craw[core] + psum_in[0]
+        cbuf[par, 0, chip] = mine
 
         def c_copy(g, off, to, src, k):
             return pltpu.make_async_remote_copy(
-                src_ref=craw.at[to], dst_ref=cbuf.at[par, g, src],
+                src_ref=cbuf.at[par, 0, chip], dst_ref=cbuf.at[par, g, src],
                 send_sem=csend.at[g, k], recv_sem=crecv.at[par, g, src],
-                device_id={"chan": to, "slot": lax.rem(slot + off, slots)},
+                device_id={"chan": 2 * to + core, "slot": lax.rem(slot + off, slots)},
                 device_id_type=pl.DeviceIdType.MESH,
             )
 
         groups = [0] + offs
-        for k in range(n - 1, -1, -1):
+        for k in range(chips - 1, -1, -1):
             for g, off in reversed(list(enumerate(groups))):
                 if k or off:
-                    c_copy(g, off, partner(k), me, k).start()
-        drain(1, bbuf)
+                    c_copy(g, off, partner(2 * k) // 2, chip, k).start()
         for g, off in enumerate(groups):
-
-            def wait_one(k, c, g=g, off=off):
-                c_copy(g, off, peer(k), peer(k), k).wait_recv()
-                return c
-
-            lax.fori_loop(1 if off == 0 else 0, n, wait_one, 0)
-        smooth = total(cbuf.at[par, 0])
+            for k in range(0 if off else 1, chips):
+                src = lax.rem(chip + k, chips)
+                c_copy(g, off, src, src, k).wait_recv()
+
+        def chip_total(g):
+            value = cbuf[par, g, 0]
+            for j in range(1, chips):
+                value = value + cbuf[par, g, j]
+            return value
+
+        smooth = chip_total(0)
         for g, off in enumerate(groups):
             if off:
                 source = lax.rem(slot - off + slots, slots)
                 near = jnp.abs(source - slot) == 1
-                smooth = smooth + total(cbuf.at[par, g]) * jnp.where(near, SMOOTHING, 0.0)
-        dbuf[me] = smooth / (1.0 + SMOOTHING * neighbours)
-        gather_start(2, dbuf)
+                smooth = smooth + chip_total(g) * jnp.where(near, SMOOTHING, 0.0)
+        dbuf[core] = smooth / (1.0 + SMOOTHING * neighbours)
+        swap(1, dbuf.at[core], dbuf.at[core]).start()
         for g, off in enumerate(groups):
-
-            def drain_one(k, c, g=g, off=off):
-                c_copy(g, off, peer(k), peer(k), k).wait_send()
-                return c
-
-            lax.fori_loop(1 if off == 0 else 0, n, drain_one, 0)
-        receive(2, dbuf)
-        coef = jnp.concatenate([dbuf[j] for j in range(n)], axis=1)
+            for k in range(0 if off else 1, chips):
+                c_copy(g, off, chip, chip, k).wait_send()
+        swap(1, dbuf.at[core], dbuf.at[1 - core]).wait()
+        coef = jnp.concatenate(
+            [dbuf[h, q : q + 1, :] for h in range(2) for q in range(half // LANES)], axis=1
+        )
         coef_out[...] = coef
         wide = [
             jnp.broadcast_to(coef[:, q * LANES : (q + 1) * LANES], (8, LANES))
@@ -375,14 +397,15 @@
         ]
 
         def screen_step(i, c):
-            at = pl.ds(pl.multiple_of(i * 8, 8), 8)
-            value = basis[at, 0:LANES] * wide[0]
-            for q in range(1, kk // LANES):
-                value = value + basis[at, q * LANES : (q + 1) * LANES] * wide[q]
-            target[at, :] = value
+            for part in range(burst):
+                at = pl.ds(pl.multiple_of((i * burst + part) * 8, 8), 8)
+                value = basis[at, 0:LANES] * wide[0]
+                for q in range(1, kk // LANES):
+                    value = value + basis[at, q * LANES : (q + 1) * LANES] * wide[q]
+                target[at, :] = value
             return c
 
-        lax.fori_loop(0, rows // 8, screen_step, 0)
+        lax.fori_loop(0, rows // 8 // burst, screen_step, 0)
         if whole8 < rows:
             value = basis[whole8:rows, 0:LANES] * wide[0][0 : rows - whole8]
             for q in range(1, kk // LANES):
@@ -400,7 +423,6 @@
         split_out(placed[0:sp] + placed[sp : 2 * sp] + placed[2 * sp : 3 * sp])
         scatter_start(4, ebuf)
         ebuf[me] = stage[me]
-        drain(2, dbuf)
         receive(4, ebuf)
         fbuf[me] = total(ebuf)
         gather_start(3, fbuf)
@@ -436,8 +458,7 @@
     sp = round_up(stations, 64)
     cr = sp * (dp // LANES) // n
     rpad = round_up(rows + 1, 16)
-    cw = kk // n
-    assert cr * n == sp * (dp // LANES) and cw * n == kk and kk % LANES == 0
+    assert cr * n == sp * (dp // LANES) and n % 2 == 0 and kk % (2 * LANES) == 0
     groups = 1 + len({1 % slots, (slots - 1) % slots} - {0})
 
     own = lax.dynamic_slice_in_dim(
@@ -445,7 +466,7 @@
     )
     f32, bf16 = jnp.float32, jnp.bfloat16
     vmem = pl.BlockSpec(memory_space=pltpu.VMEM)
-    geo = (n, slots, tiles, base_n, srcs, drows, sp, dp, cr, rows, rpad, kk, cw)
+    geo = (n, slots, tiles, base_n, srcs, drows, sp, dp, cr, rows, rpad, kk)
     tec_final, coefficients, res_re, res_im = pl.pallas_call(
         functools.partial(solve_kernel, geo),
         out_shape=(
@@ -490,16 +511,19 @@
             pltpu.VMEM((n, cr, LANES), f32),
             pltpu.VMEM((n, cr, LANES), f32),
             pltpu.VMEM((n, cr, LANES), f32),
-            pltpu.VMEM((n, 1, cw), f32),
-            pltpu.VMEM((2, groups, n, 1, cw), f32),
-            pltpu.VMEM((n, 1, cw), f32),
+            pltpu.VMEM((2, kk // 2 // LANES, LANES), f32),
+            pltpu.VMEM((2, groups, n // 2, kk // 2 // LANES, LANES), f32),
+            pltpu.VMEM((2, kk // 2 // LANES, LANES), f32),
             pltpu.VMEM((n, cr, LANES), f32),
             pltpu.VMEM((n, cr, LANES), f32),
+            pltpu.VMEM((1, kk // 2 // LANES, LANES), f32),
             pltpu.SemaphoreType.DMA,
             pltpu.SemaphoreType.DMA((5, n)),
             pltpu.SemaphoreType.DMA((5, n)),
-            pltpu.SemaphoreType.DMA((groups, n)),
-            pltpu.SemaphoreType.DMA((2, groups, n)),
+            pltpu.SemaphoreType.DMA((groups, n // 2)),
+            pltpu.SemaphoreType.DMA((2, groups, n // 2)),
+            pltpu.SemaphoreType.DMA((2,)),
+            pltpu.SemaphoreType.DMA((2,)),
         ],
         compiler_params=pltpu.CompilerParams(
             collective_id=0, has_side_effects=True, vmem_limit_bytes=60 * 1024 * 1024

time: 152 us -> 136 us (0.89)
  Pallas kernels: 144 us -> 129 us
    pallas_call x1, Pallas kernels: 144 us -> 129 us  [per_device(): pl.pallas_call(functools.partial(solve_kernel, geo), out_shape=(jax.Shape...]
where the time goes in v3:
time: 136 us
  Pallas kernels  129 us (95%)
  local copies, waits for them, and re-layouts  6.13 us (5%)
    pallas_call x1, Pallas kernels, per_device(): pl.pallas_call(functools.partial(solve_kernel, geo), out_shape=(jax.Shape...  129 us
    unnamed x6, local copies, waits for them, and re-layouts  5.48 us

profile of v3, /device:TPU:0, one launch (start us, length us, event | category | flops | bytes accessed | tf_op | source)
XLA Modules:
  0.0 136.0 jit_solution(15971862044404336389)
XLA Ops:
  0.6 0.0 copy-start
  1.3 0.1 copy-done
  1.4 0.7 constant_dynamic-slice_fusion.own_ref
  2.1 128.5 %shard_map.147 = (f32[60,1,200]{2,1,0:T(1,128)}, f32[1,2048]{1,0:T(1,128)}, f32[1,1,1770]{2,1,0:T(1,128)}, f32[1,1,1770]{2,1,0:T(1,128)}) custom-call(f32[1,1,1770]{2,1,0:T(1,128)} %vr_ref.1, f32[1,1,1770]{2,1,0:T(1,128)} %vi_ref.1, f32[1,1,1770]{2,1,0:T(1,128)} %w_ref.1, f32[3,1,1770]{2,1,0:T(1,128)} %bitcast.6, s32[2,1770]{1,0:T(2,128)} %pairs_ref.1, ...), custom_call_target="tpu_custom_call" | custom-call | tf_op jit(solution)/shard_map/pallas_call | solution.py:470
  130.6 1.5 %copy.21 = f32[1,60,200]{2,0,1:T(1,128)} copy(f32[1,60,200]{2,0,1:T(1,128)} %bitcast.4) | data formatting | bytes 96000
  132.1 1.3 copy.22
  133.4 1.3 copy.23
  134.7 1.3 copy.24
Async XLA Ops:
  0.6 0.8 copy-start
